TPU v7x, 32 devices: a whole 2x2x4 slice. The times are simulated.
32 devices in a mesh: dp: 32 (over z, y, x, core).
Axes of the slice: x: 2, y: 2, z: 4, core: 2. Of those that a mesh axis runs over, the one named last changes fastest.
Arguments:
- tokens: bfloat16 [4096, 1088], P('dp'), may hold values from -6 to 6
- seq_lengths: int32 [8], replicated, may hold values from 1 to 1024, as said below
- w_qkv: bfloat16 [3551232], P('dp'), may hold values from -8 to 8
- w_out: bfloat16 [1183744], P('dp'), may hold values from -0.75 to 0.75
- w_up: bfloat16 [4734976], P('dp'), may hold values from -0.1875 to 0.1875
- w_down: bfloat16 [4734976], P('dp'), may hold values from -0.09375 to 0.09375
- vectors: bfloat16 [16384], P('dp'), may hold values from -4 to 4
- cotangent: bfloat16 [4096, 1088], P('dp'), may hold values from -6 to 6
Outputs:
- out_block: bfloat16 [4096, 1088], P('dp')
- grad_tokens: float32 [4096, 1088], P('dp')
- grad_w_qkv: float32 [3551232], P('dp')
- grad_w_out: float32 [1183744], P('dp')
- grad_w_up: float32 [4734976], P('dp')
- grad_w_down: float32 [4734976], P('dp')
- grad_vectors: float32 [16384], P('dp')
Inputs may be any that keep to these rules, and one draw needn't show every extreme that they name: `seq_lengths`: sequences are packed end to end, each padded to whole blocks of 128 tokens, and together they fill exactly 32 blocks; a sequence covers at most 8 blocks, and some sequence covers exactly 8 full blocks.
All inputs are finite; a program needn't handle non-finite values.
Results may differ from a plain program's by a relative error of at most 0.0084.
Values may be sent and summed in bfloat16 or wider, within the bound.
A program may use at most 256 MiB of HBM per device.

v0:
```python
import jax
import jax.numpy as jnp
from jax import lax
from jax.sharding import PartitionSpec as P

D = 1088
HEADS = 17
HEAD = 64
FF = 4352
BLOCK = 128
MAXB = 8


EPS = 1e-05


def shifted(value, axis, steps):
    count = lax.axis_size(axis)
    first, last = (max(0, -steps), min(count, count - steps))
    return lax.ppermute(value, axis, [(source, source + steps) for source in range(first, last)])


def block_layout(seq_lengths, block_ids):
    counts = (seq_lengths + BLOCK - 1) // BLOCK
    end_pos = jnp.cumsum(counts)
    start_pos = end_pos - counts
    owns_block = (block_ids[:, None] >= start_pos[None, :]) & (
        block_ids[:, None] < end_pos[None, :]
    )
    first_blk = jnp.sum(jnp.where(owns_block, start_pos[None, :], 0), axis=1)
    seq_len = jnp.sum(jnp.where(owns_block, seq_lengths[None, :], 0), axis=1)
    inside = block_ids - first_blk
    filled = jnp.clip(seq_len - inside * BLOCK, 0, BLOCK)
    return (inside, filled)


def window_mask(inside):
    row_ids = jnp.arange(BLOCK, dtype=jnp.int32)[:, None]
    col_ids = jnp.arange(MAXB * BLOCK, dtype=jnp.int32)[None, :]
    slot_ids = col_ids // BLOCK
    return (slot_ids <= inside) & ((slot_ids > 0) | (col_ids <= row_ids))


def layer_norm(values, gain_vec, bias_vec):
    average = jnp.mean(values, axis=-1, keepdims=True)
    centred = values - average
    variance = jnp.mean(centred * centred, axis=-1, keepdims=True)
    inv_std = lax.rsqrt(variance + EPS)
    normalized = centred * inv_std
    return (normalized * gain_vec + bias_vec, normalized, inv_std)


def norm_back(grad_out, normalized, inv_std, gain_vec):
    grad_hat = grad_out * gain_vec
    first_mean = jnp.mean(grad_hat, axis=-1, keepdims=True)
    second_mean = jnp.mean(grad_hat * normalized, axis=-1, keepdims=True)
    return inv_std * (grad_hat - first_mean - normalized * second_mean)


def split_heads(matrix):
    return matrix.reshape(matrix.shape[0], HEADS, HEAD).transpose(1, 0, 2)


def join_heads(matrix):
    return matrix.transpose(1, 0, 2).reshape(matrix.shape[1], HEADS * HEAD)


def head_forward(query, keys, values, allowed):
    scores = jnp.dot(query, keys.T, preferred_element_type=jnp.float32)
    scores = jnp.where(allowed, scores, -1e30)
    row_max = jnp.max(scores, axis=-1)
    row_total = jnp.sum(jnp.exp(scores - row_max[:, None]), axis=-1)
    log_sums = row_max + jnp.log(row_total)
    prob_bf = jnp.where(allowed, jnp.exp(scores - log_sums[:, None]), 0.0).astype(jnp.bfloat16)
    output = jnp.dot(prob_bf, values, preferred_element_type=jnp.float32).astype(jnp.bfloat16)
    return (output, log_sums)


def head_backward(query, keys, values, output, grad_output, log_sums, allowed):
    scores = jnp.dot(query, keys.T, preferred_element_type=jnp.float32)
    probs = jnp.where(allowed, jnp.exp(scores - log_sums[:, None]), 0.0)
    prob_bf = probs.astype(jnp.bfloat16)
    grad_value = jnp.dot(prob_bf.T, grad_output, preferred_element_type=jnp.float32)
    grad_prob = jnp.dot(grad_output, values.T, preferred_element_type=jnp.float32)
    row_delta = jnp.sum(grad_output.astype(jnp.float32) * output.astype(jnp.float32), axis=-1)
    grad_score = (probs * (grad_prob - row_delta[:, None])).astype(jnp.bfloat16)
    grad_query = jnp.dot(grad_score, keys, preferred_element_type=jnp.float32)
    grad_key = jnp.dot(grad_score.T, query, preferred_element_type=jnp.float32)
    return (grad_query, grad_key, grad_value)


def attend(query, keys, values, allowed):

    def one_head(packed):
        return head_forward(packed[0], packed[1], packed[2], allowed)

    outputs, log_sums = lax.map(
        one_head, (split_heads(query), split_heads(keys), split_heads(values))
    )
    return (join_heads(outputs), log_sums)


def attend_back(query, keys, values, output, grad_output, log_sums, allowed):

    def one_head(packed):
        return head_backward(
            packed[0], packed[1], packed[2], packed[3], packed[4], packed[5], allowed
        )

    grad_query, grad_key, grad_value = lax.map(
        one_head,
        (
            split_heads(query),
            split_heads(keys),
            split_heads(values),
            split_heads(output),
            split_heads(grad_output),
            log_sums,
        ),
    )
    return (join_heads(grad_query), join_heads(grad_key), join_heads(grad_value))


def unpack(gathered):
    weight_qkv = gathered[0][: 3 * D * D].reshape(D, 3 * D)
    weight_out = gathered[1][: D * D].reshape(D, D)
    weight_up = gathered[2][: D * FF].reshape(D, FF)
    weight_down = gathered[3][: FF * D].reshape(FF, D)
    vector_rows = gathered[4][: 12 * D].reshape(12, D).astype(jnp.float32)
    return (weight_qkv, weight_out, weight_up, weight_down, vector_rows)


def pad_flat(matrix, length):
    flat = matrix.reshape(-1)
    return jnp.concatenate([flat, jnp.zeros((length - flat.shape[0],), jnp.float32)])


def local(tokens, seq_lengths, w_qkv, w_out, w_up, w_down, vectors, cotangent):
    device_pos = lax.axis_index("dp")
    inside_all, filled_all = block_layout(seq_lengths, jnp.reshape(device_pos, (1,)))
    inside = inside_all[0]
    valid = jnp.arange(BLOCK, dtype=jnp.int32) < filled_all[0]
    allowed = window_mask(inside)
    gathered = (
        lax.all_gather(w_qkv, "dp", axis=0, tiled=True),
        lax.all_gather(w_out, "dp", axis=0, tiled=True),
        lax.all_gather(w_up, "dp", axis=0, tiled=True),
        lax.all_gather(w_down, "dp", axis=0, tiled=True),
        lax.all_gather(vectors, "dp", axis=0, tiled=True),
    )
    weight_qkv, weight_out, weight_up, weight_down, vector_rows = unpack(gathered)
    qkv_length = gathered[0].shape[0]
    out_length = gathered[1].shape[0]
    ff_length = gathered[2].shape[0]
    vec_length = gathered[4].shape[0]
    bias_up = vector_rows[8:12].reshape(FF)
    query_scale = HEAD ** (-0.5)
    inputs = tokens.astype(jnp.float32)
    normed_attn, hat_one, inv_one = layer_norm(inputs, vector_rows[0], vector_rows[1])
    normed_attn = normed_attn.astype(jnp.bfloat16)
    projected = jnp.dot(normed_attn, weight_qkv, preferred_element_type=jnp.float32)
    query = (query_scale * (projected[:, :D] + vector_rows[2])).astype(jnp.bfloat16)
    keys = projected[:, D : 2 * D].astype(jnp.bfloat16)
    values = (projected[:, 2 * D :] + vector_rows[3]).astype(jnp.bfloat16)
    key_value = jnp.stack([keys, values])
    pieces = [key_value]
    for offset in range(1, MAXB):
        pieces.append(shifted(key_value, "dp", offset))
    window_kv = jnp.stack(pieces)
    window_k = window_kv[:, 0].reshape(MAXB * BLOCK, D)
    window_v = window_kv[:, 1].reshape(MAXB * BLOCK, D)
    attended, log_sums = attend(query, window_k, window_v, allowed)
    residual = (
        inputs + jnp.dot(attended, weight_out, preferred_element_type=jnp.float32) + vector_rows[4]
    )
    normed_mlp, hat_two, inv_two = layer_norm(residual, vector_rows[5], vector_rows[6])
    normed_mlp = normed_mlp.astype(jnp.bfloat16)
    up_pre = jnp.dot(normed_mlp, weight_up, preferred_element_type=jnp.float32) + bias_up
    normal_cdf = 0.5 * (1.0 + lax.erf(up_pre * 2.0 ** (-0.5)))
    activated = (up_pre * normal_cdf).astype(jnp.bfloat16)
    result = (
        residual
        + jnp.dot(activated, weight_down, preferred_element_type=jnp.float32)
        + vector_rows[7]
    )
    out_block = jnp.where(valid[:, None], result, 0.0).astype(jnp.bfloat16)
    cot_rows = jnp.where(valid[:, None], cotangent.astype(jnp.float32), 0.0)
    cot_bf = cot_rows.astype(jnp.bfloat16)
    grad_down = jnp.dot(activated.T, cot_bf, preferred_element_type=jnp.float32)
    grad_bias_down = jnp.sum(cot_rows, axis=0)
    grad_act = jnp.dot(cot_bf, weight_down.T, preferred_element_type=jnp.float32)
    normal_pdf = jnp.exp(-0.5 * up_pre * up_pre) * (2.0 * jnp.pi) ** (-0.5)
    grad_pre = grad_act * (normal_cdf + up_pre * normal_pdf)
    grad_pre_bf = grad_pre.astype(jnp.bfloat16)
    grad_up = jnp.dot(normed_mlp.T, grad_pre_bf, preferred_element_type=jnp.float32)
    grad_bias_up = jnp.sum(grad_pre, axis=0)
    grad_normed_mlp = jnp.dot(grad_pre_bf, weight_up.T, preferred_element_type=jnp.float32)
    grad_gain_two = jnp.sum(grad_normed_mlp * hat_two, axis=0)
    grad_bias_two = jnp.sum(grad_normed_mlp, axis=0)
    grad_residual = cot_rows + norm_back(grad_normed_mlp, hat_two, inv_two, vector_rows[5])
    grad_bias_out = jnp.sum(grad_residual, axis=0)
    grad_res_bf = grad_residual.astype(jnp.bfloat16)
    grad_out = jnp.dot(attended.T, grad_res_bf, preferred_element_type=jnp.float32)
    grad_attended = jnp.dot(grad_res_bf, weight_out.T, preferred_element_type=jnp.float32).astype(
        jnp.bfloat16
    )
    grad_query, grad_key, grad_value = attend_back(
        query, window_k, window_v, attended, grad_attended, log_sums, allowed
    )
    window_grads = jnp.stack(
        [grad_key.reshape(MAXB, BLOCK, D), grad_value.reshape(MAXB, BLOCK, D)], axis=1
    )
    own_grads = window_grads[0]
    for offset in range(1, MAXB):
        own_grads = own_grads + shifted(window_grads[offset], "dp", -offset)
    grad_query = query_scale * grad_query
    grad_project = jnp.concatenate([grad_query, own_grads[0], own_grads[1]], axis=1).astype(
        jnp.bfloat16
    )
    grad_bias_q = jnp.sum(grad_query, axis=0)
    grad_bias_v = jnp.sum(own_grads[1], axis=0)
    grad_qkv = jnp.dot(normed_attn.T, grad_project, preferred_element_type=jnp.float32)
    grad_normed_attn = jnp.dot(grad_project, weight_qkv.T, preferred_element_type=jnp.float32)
    grad_gain_one = jnp.sum(grad_normed_attn * hat_one, axis=0)
    grad_bias_one = jnp.sum(grad_normed_attn, axis=0)
    grad_tokens = grad_residual + norm_back(grad_normed_attn, hat_one, inv_one, vector_rows[0])
    grad_vectors = jnp.concatenate(
        [
            jnp.stack(
                [
                    grad_gain_one,
                    grad_bias_one,
                    grad_bias_q,
                    grad_bias_v,
                    grad_bias_out,
                    grad_gain_two,
                    grad_bias_two,
                    grad_bias_down,
                ]
            ),
            grad_bias_up.reshape(4, D),
        ],
        axis=0,
    )
    shard_qkv, shard_out, shard_up, shard_down, shard_vec = (
        lax.psum_scatter(pad_flat(grad_qkv, qkv_length), "dp", scatter_dimension=0, tiled=True),
        lax.psum_scatter(pad_flat(grad_out, out_length), "dp", scatter_dimension=0, tiled=True),
        lax.psum_scatter(pad_flat(grad_up, ff_length), "dp", scatter_dimension=0, tiled=True),
        lax.psum_scatter(pad_flat(grad_down, ff_length), "dp", scatter_dimension=0, tiled=True),
        lax.psum_scatter(pad_flat(grad_vectors, vec_length), "dp", scatter_dimension=0, tiled=True),
    )
    return (out_block, grad_tokens, shard_qkv, shard_out, shard_up, shard_down, shard_vec)


def solution(mesh):
    in_specs = (P("dp", None), P(), P("dp"), P("dp"), P("dp"), P("dp"), P("dp"), P("dp", None))
    out_specs = (P("dp", None), P("dp", None), P("dp"), P("dp"), P("dp"), P("dp"), P("dp"))
    return jax.shard_map(local, mesh=mesh, in_specs=in_specs, out_specs=out_specs, check_vma=False)
```

profile of v0, /device:TPU:0, one launch (start us, length us, event | category | flops | bytes accessed | tf_op | source)
XLA Modules:
  0.0 2118.6 jit_solution(10395779790932594574)
XLA Ops:
  11.0 4.4 reshape.263
  15.5 4.1 reshape.261
  19.7 44.4 %all-gather = bf16[32,1,512]{2,1,0:T(2,128)(2,1)S(1)} all-gather(bf16[1,1,512]{2,1,0:T(2,128)(2,1)S(1)} %reshape.255), channel_id=1, replica_groups=mesh['dp'=32] {'dp'}, dimensions={0}, use_global_device_ids=true | all-gather | bytes 33792 | tf_op jit(solution)/shard_map/all_gather | solution.py:149
  65.5 51.6 %all-gather.10.cloned.1.call-done = bf16[32,1,110976]{2,1,0:T(2,128)(2,1)} async-done(((bf16[1,1,110976]{2,1,0:T(2,128)(2,1)}), bf16[32,1,110976]{2,1,0:T(2,128)(2,1)}) %all-gather.10.cloned.1.call-update) | async-done | bytes 7102480 | tf_op jit(solution)/shard_map/all_gather | solution.py:145
  117.2 130.0 %reduce.8 = bf16[32,110976]{1,0:T(8,128)(2,1)} reduce(bf16[32,1,110976]{2,1,0:T(2,128)(2,1)} %all-gather.10.cloned.1.call-done, bf16[]{:T(256)} %constant.138), dimensions={1}, to_apply=%all-gather.1.reduce_sub_computation | reduce | bytes 14204930 | tf_op jit(solution)/shard_map/all_gather | solution.py:145
  247.2 9.8 reshape.238
  257.0 6.5 fusion.105
  265.4 3.0 collective-permute-start
  270.3 51.1 %reduce.9 = bf16[32,36992]{1,0:T(8,128)(2,1)} reduce(bf16[32,1,36992]{2,1,0:T(2,128)(2,1)} %all-gather.12.cloned.1.call-done, bf16[]{:T(256)} %constant.138), dimensions={1}, to_apply=%all-gather.2.reduce_sub_computation | reduce | bytes 4734978 | tf_op jit(solution)/shard_map/all_gather | solution.py:146
  321.4 4.1 reshape.241
  325.5 3.3 collective-permute-start.1
  329.6 3.3 collective-permute-start.2
  332.9 3.6 collective-permute-start.3
  339.9 4.2 collective-permute-start.5
  346.0 9.9 collective-permute-start.6
  359.8 7.1 collective-permute-done.3
  368.8 12.5 collective-permute-done.4
  383.0 5.6 collective-permute-done.6
  389.5 4.0 fusion.110
  393.4 7.8 copy.43
  401.2 4.7 reshape_reshape_squeeze.8
  405.9 5.2 copy.45
  411.2 7.1 copy.44
  418.2 4.7 reshape_reshape_squeeze.9
  422.9 5.3 copy.46
  428.2 49.0 %while.28 = (s32[]{:T(128)}, bf16[17,128,64]{1,2,0:T(8,128)(2,1)S(1)}, f32[17,128]{1,0:T(8,128)S(1)}, bf16[17,128,64]{2,1,0:T(8,128)(2,1)}, bf16[17,1024,64]{2,1...) while((s32[]{:T(128)}, ...), condition=%wide.region_8.9_spmd.clone, body=%wide.region_5.8_spmd.clone.sunk | while | flops 35266432 | bytes 2157169 | solution.py:97
  480.2 156.2 %reduce.11 = bf16[32,147968]{1,0:T(8,128)(2,1)} reduce(bf16[32,1,147968]{2,1,0:T(2,128)(2,1)} %all-gather.16.cloned.1.call-done, bf16[]{:T(256)} %constant.138), dimensions={1}, to_apply=%all-gather.4.reduce_sub_computation | reduce | bytes 18939906 | tf_op jit(solution)/shard_map/all_gather | solution.py:148
  636.4 11.8 reshape.243
  648.3 156.5 %reduce.10 = bf16[32,147968]{1,0:T(8,128)(2,1)} reduce(bf16[32,1,147968]{2,1,0:T(2,128)(2,1)} %all-gather.14.cloned.1.call-done, bf16[]{:T(256)} %constant.138), dimensions={1}, to_apply=%all-gather.3.reduce_sub_computation | reduce | bytes 18939906 | tf_op jit(solution)/shard_map/all_gather | solution.py:147
  804.8 17.3 reshape.242
  822.1 5.6 convolution_add_fusion
  827.7 7.6 fusion.113
  841.5 133.2 %while.29 = (s32[]{:T(128)}, f32[17,128,64]{1,2,0:T(8,128)}, f32[17,1024,64]{1,2,0:T(8,128)}, f32[17,1024,64]{1,2,0:T(8,128)}, bf16[17,128,64]{2,1,0:T(8,128)(2,...) while((s32[]{:T(128)}, f32[17,128,64]{1,2,0:T(8,128)}, ...), condition=%wide.region_15.16_spmd.clone, body=%wide.region_13.15_spmd.clone.sunk | while | flops 85098368 | bytes 3942033 | solution.py:110
  974.7 3.3 copy.69
  985.2 28.0 %fusion.109 = (f32[1,2,128,1088]{2,0,3,1:T(1,128)}, f32[1,2,128,1088]{2,0,3,1:T(1,128)}, f32[1,2,128,1088]{2,0,3,1:T(1,128)}, f32[1,2,128,1088]{2,0,3,1:T(1,128)...) fusion(f32[8,2,128,1088]{2,0,3,1:T(8,128)} %constant_dynamic-up, ...), kind=kLoop, calls=%fused_computation.180 | loop fusion | bytes 17825792 | tf_op jit(solution)/shard_map/slice | solution.py:215
  1019.9 8.2 fusion.77
  1028.1 86.2 %collective-permute-done.13 = f32[2,128,1088]{1,2,0:T(8,128)S(1)} collective-permute-done((f32[2,128,1088]{1,2,0:T(8,128)}, f32[2,128,1088]{1,2,0:T(8,128)S(1)}, u32[]{:S(2)}, u32[]{:S(2)}) %collective-permute-start.13) | collective-permute-done | bytes 1114144 | tf_op jit(solution)/shard_map/ppermute | solution.py:20
  1118.8 3.1 fusion.92
  1121.9 6.9 reshape.246
  1128.8 20.0 reshape.247
  1148.8 8.3 fusion.89
  1157.1 23.5 %reshape.248 = f32[4734976]{0:T(1024)} reshape(f32[4352,1088]{1,0:T(8,128)} %fusion.89) | data formatting | bytes 37879808 | tf_op jit(solution)/shard_map/reshape | solution.py:134
  1182.1 4.0 add_add_fusion
  1186.2 5.9 fusion.72
  1192.1 7.4 fusion.83
  1199.7 17.8 reshape.245
  1219.1 7.9 fusion.55
  1228.0 874.7 %all-reduce.9.cloned.1.call-done = (f32[3551232]{0:T(1024)}, f32[1183744]{0:T(1024)}, f32[4734976]{0:T(1024)}, f32[4734976]{0:T(1024)}, f32[16384]{0:T(1024)}) async-done(((f32[3551232]{0:T(1024)}, f32[1183744]{0:T(1024)}, f32[4734976]{0:T(1024)}, f32[4734976]{0:T(1024)}, f32[16384]{0:T(1024)}), (f32[3551232]{0:T(1024)}, f32[1183744]{0:T(1024)}, f32[4734976]{0:T(1024)}, f32[4734976]{0:T(1024)}, ...) | async-done | bytes 56885264
  (389 shorter events, 244.6 us)
Async XLA Ops:
  7.2 8.3 copy-start.15
  7.2 12.5 copy-start.17
  7.2 110.0 %all-gather.10.cloned.1.call-start = ((), (), s32[]{:S(2)}) async-start(), calls=%async_computation | async-start | bytes 14648832 | tf_op jit(solution)/shard_map/all_gather | solution.py:145
  9.2 55.8 %copy-start.2 = (bf16[128,1088]{0,1:T(8,128)(2,1)S(1)}, bf16[128,1088]{0,1:T(8,128)(2,1)}, u32[]{:S(2)}) copy-start(bf16[128,1088]{0,1:T(8,128)(2,1)} %param.12) | copy-start | bytes 835588
  9.2 56.1 %copy-start.18 = (s32[8]{0:T(128)S(1)}, s32[8]{0:T(128)}, u32[]{:S(2)}) copy-start(s32[8]{0:T(128)} %param.13) | copy-start | bytes 100
  9.2 261.1 %all-gather.12.cloned.1.call-start = ((), (), s32[]{:S(2)}) async-start(), calls=%async_computation.1 | async-start | bytes 4882944 | tf_op jit(solution)/shard_map/all_gather | solution.py:146
  10.9 469.3 %all-gather.16.cloned.1.call-start = ((), (), s32[]{:S(2)}) async-start(), calls=%async_computation.3 | async-start | bytes 19531776 | tf_op jit(solution)/shard_map/all_gather | solution.py:148
  15.4 632.8 %all-gather.14.cloned.1.call-start = ((), (), s32[]{:S(2)}) async-start(), calls=%async_computation.2 | async-start | bytes 19531776 | tf_op jit(solution)/shard_map/all_gather | solution.py:147
  19.6 2083.1 %all-reduce.9.cloned.1.call-start = ((), (), s32[]{:S(2)}) async-start(), calls=%async_computation.4 | async-start | bytes 113770496
  265.4 74.5 %collective-permute-start = (bf16[2,128,1088]{1,2,0:T(8,128)(2,1)}, bf16[2,128,1088]{1,2,0:T(8,128)(2,1)}, u32[]{:S(2)}, u32[]{:S(2)}) collective-permute-start(bf16[2,128,1088]{1,2,0:T(8,128)(2,1)} %pad_maximum_fusion.1), channel_id=1, source_target_pairs={{0,1},{1,2},{2,3},{3,4},{4,5},{5,6},{6,7},{7,8},{8,9},{9,10},{10,1... | collective-permute-start | bytes 1671176 | tf_op jit(solution)/shard_map/ppermute | solution.py:20
  325.5 20.5 collective-permute-start.1
  329.6 28.3 %collective-permute-start.2 = (bf16[2,128,1088]{1,2,0:T(8,128)(2,1)}, bf16[2,128,1088]{1,2,0:T(8,128)(2,1)}, u32[]{:S(2)}, u32[]{:S(2)}) collective-permute-start(bf16[2,128,1088]{1,2,0:T(8,128)(2,1)} %pad_maximum_fusion.1), channel_id=1, source_target_pairs={{0,3},{1,4},{2,5},{3,6},{4,7},{5,8},{6,9},{7,10},{8,11},{9,12},{10... | collective-permute-start | bytes 1671176 | tf_op jit(solution)/shard_map/ppermute | solution.py:20
  332.9 34.0 %collective-permute-start.3 = (bf16[2,128,1088]{1,2,0:T(8,128)(2,1)}, bf16[2,128,1088]{1,2,0:T(8,128)(2,1)}, u32[]{:S(2)}, u32[]{:S(2)}) collective-permute-start(bf16[2,128,1088]{1,2,0:T(8,128)(2,1)} %pad_maximum_fusion.1), channel_id=1, source_target_pairs={{0,4},{1,5},{2,6},{3,7},{4,8},{5,9},{6,10},{7,11},{8,12},{9,13},{1... | collective-permute-start | bytes 1671176 | tf_op jit(solution)/shard_map/ppermute | solution.py:20
  336.5 44.8 %collective-permute-start.4 = (bf16[2,128,1088]{1,2,0:T(8,128)(2,1)}, bf16[2,128,1088]{1,2,0:T(8,128)(2,1)S(1)}, u32[]{:S(2)}, u32[]{:S(2)}) collective-permute-start(bf16[2,128,1088]{1,2,0:T(8,128)(2,1)} %pad_maximum_fusion.1), channel_id=1, source_target_pairs={{0,5},{1,6},{2,7},{3,8},{4,9},{5,10},{6,11},{7,12},{8,13},{9,14},{... | collective-permute-start | bytes 1671176 | tf_op jit(solution)/shard_map/ppermute | solution.py:20
  339.9 42.3 %collective-permute-start.5 = (bf16[2,128,1088]{1,2,0:T(8,128)(2,1)}, bf16[2,128,1088]{1,2,0:T(8,128)(2,1)S(1)}, u32[]{:S(2)}, u32[]{:S(2)}) collective-permute-start(bf16[2,128,1088]{1,2,0:T(8,128)(2,1)} %pad_maximum_fusion.1), channel_id=1, source_target_pairs={{0,6},{1,7},{2,8},{3,9},{4,10},{5,11},{6,12},{7,13},{8,14},{9,15},... | collective-permute-start | bytes 1671176 | tf_op jit(solution)/shard_map/ppermute | solution.py:20
  346.0 42.6 %collective-permute-start.6 = (bf16[2,128,1088]{1,2,0:T(8,128)(2,1)}, bf16[2,128,1088]{1,2,0:T(8,128)(2,1)S(1)}, u32[]{:S(2)}, u32[]{:S(2)}) collective-permute-start(bf16[2,128,1088]{1,2,0:T(8,128)(2,1)} %pad_maximum_fusion.1), channel_id=1, source_target_pairs={{0,7},{1,8},{2,9},{3,10},{4,11},{5,12},{6,13},{7,14},{8,15},{9,16}... | collective-permute-start | bytes 1671176 | tf_op jit(solution)/shard_map/ppermute | solution.py:20
  422.9 5.3 copy-start.8
  477.2 0.7 copy-start.9
  822.0 5.6 copy-start.11
  822.0 13.3 slice-start
  822.0 13.3 slice-start.1
  827.7 7.6 copy-start
  827.7 7.6 slice-start.2
  835.3 2.8 copy-start.6
  838.7 1.5 copy-start.3
  978.0 3.8 slice-start.3
  978.1 3.8 slice-start.4
  985.2 34.7 %copy-start.7 = (bf16[128,4352]{1,0:T(8,128)(2,1)S(1)}, bf16[128,4352]{1,0:T(8,128)(2,1)}, u32[]{:S(2)}) copy-start(bf16[128,4352]{1,0:T(8,128)(2,1)} %copy-done.6) | copy-start | bytes 3342340
  1013.3 101.0 %collective-permute-start.13 = (f32[2,128,1088]{1,2,0:T(8,128)}, f32[2,128,1088]{1,2,0:T(8,128)S(1)}, u32[]{:S(2)}, u32[]{:S(2)}) collective-permute-start(f32[2,128,1088]{1,2,0:T(8,128)} %bitcast.222), channel_id=1, source_target_pairs={{7,0},{8,1},{9,2},{10,3},{11,4},{12,5},{13,6},{14,7},{15,8},{16,9}... | collective-permute-start | bytes 3342344 | tf_op jit(solution)/shard_map/ppermute | solution.py:20
  1014.6 102.9 %collective-permute-start.12 = (f32[2,128,1088]{1,2,0:T(8,128)}, f32[2,128,1088]{1,2,0:T(8,128)}, u32[]{:S(2)}, u32[]{:S(2)}) collective-permute-start(f32[2,128,1088]{1,2,0:T(8,128)} %bitcast.221), channel_id=1, source_target_pairs={{6,0},{7,1},{8,2},{9,3},{10,4},{11,5},{12,6},{13,7},{14,8},{15,9},... | collective-permute-start | bytes 3342344 | tf_op jit(solution)/shard_map/ppermute | solution.py:20
  1015.9 166.2 %collective-permute-start.11 = (f32[2,128,1088]{1,2,0:T(8,128)}, f32[2,128,1088]{1,2,0:T(8,128)}, u32[]{:S(2)}, u32[]{:S(2)}) collective-permute-start(f32[2,128,1088]{1,2,0:T(8,128)} %bitcast.220), channel_id=1, source_target_pairs={{5,0},{6,1},{7,2},{8,3},{9,4},{10,5},{11,6},{12,7},{13,8},{14,9},{... | collective-permute-start | bytes 3342344 | tf_op jit(solution)/shard_map/ppermute | solution.py:20
  1017.2 164.9 %collective-permute-start.10 = (f32[2,128,1088]{1,2,0:T(8,128)}, f32[2,128,1088]{1,2,0:T(8,128)}, u32[]{:S(2)}, u32[]{:S(2)}) collective-permute-start(f32[2,128,1088]{1,2,0:T(8,128)} %bitcast.219), channel_id=1, source_target_pairs={{4,0},{5,1},{6,2},{7,3},{8,4},{9,5},{10,6},{11,7},{12,8},{13,9},{1... | collective-permute-start | bytes 3342344 | tf_op jit(solution)/shard_map/ppermute | solution.py:20
  1018.5 100.3 %copy-start.4 = (f32[128,1088]{0,1:T(8,128)S(1)}, f32[128,1088]{0,1:T(8,128)}, u32[]{:S(2)}) copy-start(f32[128,1088]{0,1:T(8,128)} %copy-done.3) | copy-start | bytes 1671172
  1018.5 100.3 %copy-start.10 = (bf16[17,128,64]{1,2,0:T(8,128)(2,1)S(1)}, bf16[17,128,64]{1,2,0:T(8,128)(2,1)}, u32[]{:S(2)}) copy-start(bf16[17,128,64]{1,2,0:T(8,128)(2,1)} %get-tuple-element.529) | copy-start | bytes 835588
  1018.5 163.6 %collective-permute-start.9 = (f32[2,128,1088]{1,2,0:T(8,128)}, f32[2,128,1088]{1,2,0:T(8,128)}, u32[]{:S(2)}, u32[]{:S(2)}) collective-permute-start(f32[2,128,1088]{1,2,0:T(8,128)} %bitcast.218), channel_id=1, source_target_pairs={{3,0},{4,1},{5,2},{6,3},{7,4},{8,5},{9,6},{10,7},{11,8},{12,9},{13... | collective-permute-start | bytes 3342344 | tf_op jit(solution)/shard_map/ppermute | solution.py:20
  1114.3 7.7 copy-start.13
  1114.3 67.9 %collective-permute-start.8 = (f32[2,128,1088]{1,2,0:T(8,128)}, f32[2,128,1088]{1,2,0:T(8,128)}, u32[]{:S(2)}, u32[]{:S(2)}) collective-permute-start(f32[2,128,1088]{1,2,0:T(8,128)} %bitcast.26), channel_id=1, source_target_pairs={{2,0},{3,1},{4,2},{5,3},{6,4},{7,5},{8,6},{9,7},{10,8},{11,9},{12,... | collective-permute-start | bytes 3342344 | tf_op jit(solution)/shard_map/ppermute | solution.py:20
  1117.5 64.6 %collective-permute-start.7 = (f32[2,128,1088]{1,2,0:T(8,128)}, f32[2,128,1088]{1,2,0:T(8,128)}, u32[]{:S(2)}, u32[]{:S(2)}) collective-permute-start(f32[2,128,1088]{1,2,0:T(8,128)} %bitcast.25), channel_id=1, source_target_pairs={{1,0},{2,1},{3,2},{4,3},{5,4},{6,5},{7,6},{8,7},{9,8},{10,9},{11,1... | collective-permute-start | bytes 3342344 | tf_op jit(solution)/shard_map/ppermute | solution.py:20
  1128.8 20.0 copy-start.1
  1128.8 20.0 copy-start.12
  1218.4 0.7 copy-start.16
  1219.1 7.9 copy-start.5
  1219.1 7.9 copy-start.14
Sparse Core Ops, SparseCore 0:
  11.5 105.6 all-gather.9
  120.6 62.0 all-gather.11
  186.3 128.5 all-gather.15
  318.2 152.9 all-gather.13
  1218.5 884.1 all-reduce.8
where the time goes:
time: 2130 us; the launch traced here: 2120 us
  waiting for transfers between devices  1040 us (49%)
  other arithmetic  511 us (24%)
  local copies, waits for them, and re-layouts  241 us (11%)
  matrix products  227 us (11%)
  blocking collectives  44.4 us (2%)
  starting transfers between devices  38 us (2%)
    unnamed x6, waiting for transfers between devices  875 us
    all_gather x1, other arithmetic, local(): lax.all_gather(w_up, 'dp', axis=0, tiled=True)  157 us
    all_gather x1, other arithmetic, local(): lax.all_gather(w_down, 'dp', axis=0, tiled=True)  156 us
    all_gather x1, other arithmetic, local(): lax.all_gather(w_qkv, 'dp', axis=0, tiled=True)  130 us
    ppermute x14, waiting for transfers between devices, shifted(): lax.ppermute(value, axis, [(source, source + steps) for source in range(f...  113 us
    reshape x5, local copies, waits for them, and re-layouts, pad_flat(): flat = matrix.reshape(-1)  68.2 us
    all_gather x1, waiting for transfers between devices, local(): lax.all_gather(w_qkv, 'dp', axis=0, tiled=True)  51.6 us
    all_gather x1, other arithmetic, local(): lax.all_gather(w_out, 'dp', axis=0, tiled=True)  51.1 us
  transfers between devices with their start and end apart: 19, of which 7 were waited for; matrix products, arithmetic and copies ran while one was open for 27% of the time, Pallas kernels for 0%

commit v1 on v0

--- a/solution.py
+++ b/solution.py
@@ -1,6 +1,7 @@
 import jax
 import jax.numpy as jnp
 from jax import lax
+from jax.experimental.layout import Layout, with_layout_constraint
 from jax.sharding import PartitionSpec as P
 
 D = 1088
@@ -12,6 +13,7 @@
 
 
 EPS = 1e-05
+WIRE = jnp.bfloat16
 
 
 def shifted(value, axis, steps):
@@ -90,49 +92,51 @@
 
 
 def attend(query, keys, values, allowed):
-
-    def one_head(packed):
-        return head_forward(packed[0], packed[1], packed[2], allowed)
-
-    outputs, log_sums = lax.map(
-        one_head, (split_heads(query), split_heads(keys), split_heads(values))
+    outputs, log_sums = jax.vmap(head_forward, (0, 0, 0, None))(
+        split_heads(query), split_heads(keys), split_heads(values), allowed
     )
     return (join_heads(outputs), log_sums)
 
 
 def attend_back(query, keys, values, output, grad_output, log_sums, allowed):
-
-    def one_head(packed):
-        return head_backward(
-            packed[0], packed[1], packed[2], packed[3], packed[4], packed[5], allowed
-        )
-
-    grad_query, grad_key, grad_value = lax.map(
-        one_head,
-        (
-            split_heads(query),
-            split_heads(keys),
-            split_heads(values),
-            split_heads(output),
-            split_heads(grad_output),
-            log_sums,
-        ),
+    grad_query, grad_key, grad_value = jax.vmap(head_backward, (0, 0, 0, 0, 0, 0, None))(
+        split_heads(query),
+        split_heads(keys),
+        split_heads(values),
+        split_heads(output),
+        split_heads(grad_output),
+        log_sums,
+        allowed,
     )
     return (join_heads(grad_query), join_heads(grad_key), join_heads(grad_value))
 
 
-def unpack(gathered):
-    weight_qkv = gathered[0][: 3 * D * D].reshape(D, 3 * D)
-    weight_out = gathered[1][: D * D].reshape(D, D)
-    weight_up = gathered[2][: D * FF].reshape(D, FF)
-    weight_down = gathered[3][: FF * D].reshape(FF, D)
-    vector_rows = gathered[4][: 12 * D].reshape(12, D).astype(jnp.float32)
-    return (weight_qkv, weight_out, weight_up, weight_down, vector_rows)
+def whole_rows(shard, rows, cols):
+    count = lax.axis_size("dp")
+    return shard.shape[0] % cols == 0 and shard.shape[0] * count == rows * cols
+
+
+def gather_matrix(shard, rows, cols):
+    if whole_rows(shard, rows, cols):
+        return lax.all_gather(shard.reshape(-1, cols), "dp", axis=0, tiled=True)
+    flat = lax.all_gather(shard, "dp", axis=0, tiled=True)
+    return flat[: rows * cols].reshape(rows, cols)
+
+
+def scatter_matrix(grad, shard):
+    rows, cols = grad.shape
+    grad = with_layout_constraint(grad.astype(WIRE), Layout((0, 1)))
+    if whole_rows(shard, rows, cols):
+        split = grad.reshape(lax.axis_size("dp"), -1, cols)
+        own = lax.psum_scatter(split, "dp", scatter_dimension=0, tiled=False)
+        return own.reshape(-1).astype(jnp.float32)
+    flat = pad_flat(grad, shard.shape[0] * lax.axis_size("dp"))
+    return lax.psum_scatter(flat, "dp", scatter_dimension=0, tiled=True).astype(jnp.float32)
 
 
 def pad_flat(matrix, length):
     flat = matrix.reshape(-1)
-    return jnp.concatenate([flat, jnp.zeros((length - flat.shape[0],), jnp.float32)])
+    return jnp.concatenate([flat, jnp.zeros((length - flat.shape[0],), flat.dtype)])
 
 
 def local(tokens, seq_lengths, w_qkv, w_out, w_up, w_down, vectors, cotangent):
@@ -141,18 +145,13 @@
     inside = inside_all[0]
     valid = jnp.arange(BLOCK, dtype=jnp.int32) < filled_all[0]
     allowed = window_mask(inside)
-    gathered = (
-        lax.all_gather(w_qkv, "dp", axis=0, tiled=True),
-        lax.all_gather(w_out, "dp", axis=0, tiled=True),
-        lax.all_gather(w_up, "dp", axis=0, tiled=True),
-        lax.all_gather(w_down, "dp", axis=0, tiled=True),
-        lax.all_gather(vectors, "dp", axis=0, tiled=True),
-    )
-    weight_qkv, weight_out, weight_up, weight_down, vector_rows = unpack(gathered)
-    qkv_length = gathered[0].shape[0]
-    out_length = gathered[1].shape[0]
-    ff_length = gathered[2].shape[0]
-    vec_length = gathered[4].shape[0]
+    vec_length = vectors.shape[0] * lax.axis_size("dp")
+    vector_rows = lax.all_gather(vectors, "dp", axis=0, tiled=True)
+    vector_rows = vector_rows[: 12 * D].reshape(12, D).astype(jnp.float32)
+    weight_qkv = gather_matrix(w_qkv, D, 3 * D)
+    weight_out = gather_matrix(w_out, D, D)
+    weight_up = gather_matrix(w_up, D, FF)
+    weight_down = gather_matrix(w_down, FF, D)
     bias_up = vector_rows[8:12].reshape(FF)
     query_scale = HEAD ** (-0.5)
     inputs = tokens.astype(jnp.float32)
@@ -204,18 +203,31 @@
     grad_attended = jnp.dot(grad_res_bf, weight_out.T, preferred_element_type=jnp.float32).astype(
         jnp.bfloat16
     )
+    grad_down, grad_up, grad_out, grad_attended = lax.optimization_barrier(
+        (grad_down.astype(WIRE), grad_up.astype(WIRE), grad_out.astype(WIRE), grad_attended)
+    )
+    shard_down = scatter_matrix(grad_down, w_down)
+    shard_up = scatter_matrix(grad_up, w_up)
+    shard_out = scatter_matrix(grad_out, w_out)
     grad_query, grad_key, grad_value = attend_back(
         query, window_k, window_v, attended, grad_attended, log_sums, allowed
     )
+    grad_query, grad_key, grad_value, shard_down = lax.optimization_barrier(
+        (grad_query, grad_key, grad_value, shard_down)
+    )
     window_grads = jnp.stack(
         [grad_key.reshape(MAXB, BLOCK, D), grad_value.reshape(MAXB, BLOCK, D)], axis=1
     )
+    sent_grads = window_grads.astype(WIRE)
     own_grads = window_grads[0]
     for offset in range(1, MAXB):
-        own_grads = own_grads + shifted(window_grads[offset], "dp", -offset)
+        own_grads = own_grads + shifted(sent_grads[offset], "dp", -offset).astype(jnp.float32)
     grad_query = query_scale * grad_query
     grad_project = jnp.concatenate([grad_query, own_grads[0], own_grads[1]], axis=1).astype(
         jnp.bfloat16
+    )
+    grad_project, shard_up, shard_out = lax.optimization_barrier(
+        (grad_project, shard_up, shard_out)
     )
     grad_bias_q = jnp.sum(grad_query, axis=0)
     grad_bias_v = jnp.sum(own_grads[1], axis=0)
@@ -242,12 +254,9 @@
         ],
         axis=0,
     )
-    shard_qkv, shard_out, shard_up, shard_down, shard_vec = (
-        lax.psum_scatter(pad_flat(grad_qkv, qkv_length), "dp", scatter_dimension=0, tiled=True),
-        lax.psum_scatter(pad_flat(grad_out, out_length), "dp", scatter_dimension=0, tiled=True),
-        lax.psum_scatter(pad_flat(grad_up, ff_length), "dp", scatter_dimension=0, tiled=True),
-        lax.psum_scatter(pad_flat(grad_down, ff_length), "dp", scatter_dimension=0, tiled=True),
-        lax.psum_scatter(pad_flat(grad_vectors, vec_length), "dp", scatter_dimension=0, tiled=True),
+    shard_qkv = scatter_matrix(grad_qkv, w_qkv)
+    shard_vec = lax.psum_scatter(
+        pad_flat(grad_vectors, vec_length), "dp", scatter_dimension=0, tiled=True
     )
     return (out_block, grad_tokens, shard_qkv, shard_out, shard_up, shard_down, shard_vec)
 

time: 2130 us -> 1100 us (0.52)
  other arithmetic: 511 us -> 18.6 us
  waiting for transfers between devices: 1040 us -> 745 us
  matrix products: 227 us -> 83.3 us
  local copies, waits for them, and re-layouts: 241 us -> 111 us
  starting transfers between devices: 38 us -> 74.6 us
    unnamed x6 -> x12, waiting for transfers between devices: 875 us -> 267 us
    all_gather x5 -> x1, other arithmetic: 494 us -> 0.18 us  [local(): vector_rows = lax.all_gather(vectors, 'dp', axis=0, tiled=True)]
    reduce_scatter x0 -> x2, waiting for transfers between devices: none -> 303 us  [scatter_matrix(): own = lax.psum_scatter(split, 'dp', scatter_dimension=0, tiled=False)]
    all_gather x4, waiting for transfers between devices: 51.7 us -> 132 us  [gather_matrix(): return lax.all_gather(shard.reshape(-1, cols), 'dp', axis=0, tiled=True)]
    ppermute x14, waiting for transfers between devices: 113 us -> 44 us  [shifted(): lax.ppermute(value, axis, [(source, source + steps) for source in range(f...]
    reshape x5 -> x1, local copies, waits for them, and re-layouts: 68.2 us -> 0.09 us  [pad_flat(): flat = matrix.reshape(-1)]
    ppermute x14, starting transfers between devices: 37.8 us -> 74.1 us  [shifted(): lax.ppermute(value, axis, [(source, source + steps) for source in range(f...]
    dot_general x17 -> x1, matrix products: 30.8 us -> 2.49 us  [head_backward(): grad_query = jnp.dot(grad_score, keys, preferred_element_type=jnp.float32)]
  transfers between devices with their start and end apart: 19 -> 23, of which waited for: 7 -> 11; matrix products, arithmetic and copies ran while one was open for 27% -> 15% of each run, Pallas kernels for 0% -> 0%
where the time goes in v1:
time: 1100 us; the launch traced here: 1090 us
  waiting for transfers between devices  745 us (68%)
  local copies, waits for them, and re-layouts  111 us (10%)
  matrix products  83.3 us (8%)
  starting transfers between devices  74.6 us (7%)
  blocking collectives  43.7 us (4%)
  other arithmetic  18.6 us (2%)
  between operations  16.1 us (1%)
    reduce_scatter x2, waiting for transfers between devices, scatter_matrix(): own = lax.psum_scatter(split, 'dp', scatter_dimension=0, tiled=False)  303 us
    unnamed x12, waiting for transfers between devices  267 us
    all_gather x4, waiting for transfers between devices, gather_matrix(): return lax.all_gather(shard.reshape(-1, cols), 'dp', axis=0, tiled=True)  132 us
    ppermute x14, starting transfers between devices, shifted(): lax.ppermute(value, axis, [(source, source + steps) for source in range(f...  74.1 us
    unnamed x82, local copies, waits for them, and re-layouts  46.6 us
    ppermute x14, waiting for transfers between devices, shifted(): lax.ppermute(value, axis, [(source, source + steps) for source in range(f...  44 us
    all_gather x1, blocking collectives, local(): vector_rows = lax.all_gather(vectors, 'dp', axis=0, tiled=True)  43.7 us
    reshape x3, local copies, waits for them, and re-layouts, scatter_matrix(): split = grad.reshape(lax.axis_size('dp'), -1, cols)  24.9 us
  transfers between devices with their start and end apart: 23, of which 11 were waited for; matrix products, arithmetic and copies ran while one was open for 15% of the time, Pallas kernels for 0%

profile of v1, /device:TPU:0, one launch (start us, length us, event | category | flops | bytes accessed | tf_op | source)
XLA Modules:
  0.0 1092.8 jit_solution(7066144278401834801)
XLA Ops:
  19.2 43.7 %all-gather = bf16[32,1,512]{2,1,0:T(2,128)(2,1)S(1)} all-gather(bf16[1,1,512]{2,1,0:T(2,128)(2,1)S(1)} %reshape.252), channel_id=1, replica_groups=mesh['dp'=32] {'dp'}, dimensions={0}, use_global_device_ids=true | all-gather | bytes 33792 | tf_op jit(solution)/shard_map/all_gather | solution.py:149
  66.1 25.9 %all-gather.11.cloned.1.call-done = bf16[32,34,3264]{2,1,0:T(8,128)(2,1)} async-done(((bf16[1,34,3264]{2,1,0:T(8,128)(2,1)}), bf16[32,34,3264]{2,1,0:T(8,128)(2,1)}) %all-gather.11.cloned.1.call-update) | async-done | bytes 7102480 | tf_op jit(solution)/shard_map/all_gather | solution.py:121
  92.0 9.9 reshape.255
  101.9 6.5 fusion.75
  109.7 3.0 collective-permute-start
  112.7 40.0 %all-gather.13.cloned.1.call-done = bf16[32,34,1088]{2,1,0:T(8,128)(2,1)} async-done(((bf16[1,34,1088]{2,1,0:T(8,128)(2,1)}), bf16[32,34,1088]{2,1,0:T(8,128)(2,1)}) %all-gather.13.cloned.1.call-update) | async-done | bytes 2367504 | tf_op jit(solution)/shard_map/all_gather | solution.py:121
  152.8 3.2 reshape.257
  156.0 3.4 collective-permute-start.5
  159.4 2.7 collective-permute-start.4
  162.1 2.5 collective-permute-start.3
  164.6 2.7 collective-permute-start.1
  168.4 3.9 collective-permute-start.2
  173.4 13.8 %collective-permute-done.1 = bf16[2,128,1088]{1,2,0:T(8,128)(2,1)S(1)} collective-permute-done((bf16[2,128,1088]{1,2,0:T(8,128)(2,1)}, bf16[2,128,1088]{1,2,0:T(8,128)(2,1)S(1)}, u32[]{:S(2)}, u32[]{:S(2)}) %collective-permute-start.1) | collective-permute-done | bytes 557088 | tf_op jit(solution)/shard_map/ppermute | solution.py:22
  187.1 46.7 %collective-permute-start.6 = (bf16[2,128,1088]{1,2,0:T(8,128)(2,1)}, bf16[2,128,1088]{1,2,0:T(8,128)(2,1)S(1)}, u32[]{:S(2)}, u32[]{:S(2)}) collective-permute-start(bf16[2,128,1088]{1,2,0:T(8,128)(2,1)} %pad_maximum_fusion.1), channel_id=1, source_target_pairs={{0,7},{1,8},{2,9},{3,10},{4,11},{5,12},{6,13},{7,14},{8,15},{9,16}... | collective-permute-start | bytes 1671176 | tf_op jit(solution)/shard_map/ppermute | solution.py:22
  234.2 18.7 %collective-permute-done.6 = bf16[2,128,1088]{1,2,0:T(8,128)(2,1)S(1)} collective-permute-done((bf16[2,128,1088]{1,2,0:T(8,128)(2,1)}, bf16[2,128,1088]{1,2,0:T(8,128)(2,1)S(1)}, u32[]{:S(2)}, u32[]{:S(2)}) %collective-permute-start.6) | collective-permute-done | bytes 557088 | tf_op jit(solution)/shard_map/ppermute | solution.py:22
  254.8 7.3 copy.21
  262.1 4.7 reshape_reshape_squeeze.8
  266.8 6.9 copy.22
  273.7 4.9 reshape_reshape_squeeze.9
  278.6 3.2 select_reduce_fusion
  285.5 2.3 fusion.22
  289.9 11.4 %reshape.259 = bf16[1088,4352]{1,0:T(8,128)(2,1)} reshape(bf16[32,34,4352]{2,1,0:T(8,128)(2,1)} %all-gather.15.cloned.1.call-done) | data formatting | bytes 18939904
  301.3 6.9 convolution_add_fusion
  308.2 65.7 %all-gather.9.cloned.1.call-done = bf16[4352,1088]{1,0:T(8,128)(2,1)} async-done(((bf16[136,1088]{1,0:T(8,128)(2,1)}), bf16[4352,1088]{1,0:T(8,128)(2,1)}) %all-gather.9.cloned.1.call-update) | async-done | bytes 9469968 | tf_op jit(solution)/shard_map/all_gather | solution.py:121
  373.9 8.1 fusion.81
  382.1 2.8 multiply_reduce_fusion
  387.7 2.3 convolution_convert_fusion.3
  390.0 5.5 convolution_convert_fusion
  395.5 5.4 convolution_convert_fusion.1
  400.9 4.4 reshape.241
  405.4 11.2 %reshape.240 = bf16[32,34,4352]{2,1,0:T(8,128)(2,1)} reshape(bf16[1088,4352]{1,0:T(8,128)(2,1)} %convolution_convert_fusion) | data formatting | bytes 18939904 | tf_op jit(solution)/shard_map/reshape | solution.py:130
  418.6 8.1 multiply_convert_fusion
  426.7 2.5 fusion.16
  429.2 3.1 fusion.82
  433.2 3.7 fusion.1
  436.9 95.8 %reduce-scatter.13.cloned.1.call-done = bf16[1,136,1088]{2,1,0:T(8,128)(2,1)} async-done(((bf16[32,136,1088]{2,1,0:T(8,128)(2,1)}), bf16[1,136,1088]{2,1,0:T(8,128)(2,1)}) %reduce-scatter.13.cloned.1.call-update) | async-done | bytes 295952
  534.8 3.5 copy.28
  541.9 2.6 copy-done.3
  553.9 11.4 %collective-permute-done.13 = bf16[2,128,1088]{1,2,0:T(8,128)(2,1)} collective-permute-done((bf16[2,128,1088]{1,2,0:T(8,128)(2,1)S(1)}, bf16[2,128,1088]{1,2,0:T(8,128)(2,1)}, u32[]{:S(2)}, u32[]{:S(2)}) %collective-permute-start.13) | collective-permute-done | bytes 557088 | tf_op jit(solution)/shard_map/ppermute | solution.py:22
  567.0 81.3 %reduce-scatter.15.cloned.1.call-done = bf16[1,34,1088]{2,1,0:T(8,128)(2,1)} async-done(((bf16[32,34,1088]{2,1,0:T(8,128)(2,1)}), bf16[1,34,1088]{2,1,0:T(8,128)(2,1)}) %reduce-scatter.15.cloned.1.call-update) | async-done | bytes 74000
  651.3 2.9 fusion.31
  655.5 150.1 %reduce-scatter.9.cloned.1.call-done = bf16[1,34,4352]{2,1,0:T(8,128)(2,1)} async-done(((bf16[32,34,4352]{2,1,0:T(8,128)(2,1)}), bf16[1,34,4352]{2,1,0:T(8,128)(2,1)}) %reduce-scatter.9.cloned.1.call-update) | async-done | bytes 295952 | tf_op jit(solution)/shard_map/reduce_scatter | solution.py:131
  807.8 6.1 fusion.44
  814.8 6.4 convolution_convert_fusion.2
  821.2 9.4 reshape.242
  831.3 7.9 fusion.11
  840.3 89.9 %all-reduce.6.cloned.1.call-done = f32[16384]{0:T(1024)} async-done(((f32[16384]{0:T(1024)}), f32[16384]{0:T(1024)}) %all-reduce.6.cloned.1.call-update) | async-done | bytes 65552
  931.5 152.6 %reduce-scatter.11.cloned.1.call-done = bf16[1,34,3264]{2,1,0:T(8,128)(2,1)} async-done(((bf16[32,34,3264]{2,1,0:T(8,128)(2,1)}), bf16[1,34,3264]{2,1,0:T(8,128)(2,1)}) %reduce-scatter.11.cloned.1.call-update) | async-done | bytes 221968 | tf_op jit(solution)/shard_map/reduce_scatter | solution.py:131
  (173 shorter events, 60.0 us)
Async XLA Ops:
  7.2 84.8 %all-gather.11.cloned.1.call-start = ((), (), s32[]{:S(2)}) async-start(), calls=%async_computation.7 | async-start | bytes 8785920 | tf_op jit(solution)/shard_map/all_gather | solution.py:121
  9.1 143.6 %all-gather.13.cloned.1.call-start = ((), (), s32[]{:S(2)}) async-start(), calls=%async_computation.8 | async-start | bytes 3041280 | tf_op jit(solution)/shard_map/all_gather | solution.py:121
  10.9 279.1 %all-gather.15.cloned.1.call-start = ((), (), s32[]{:S(2)}) async-start(), calls=%async_computation.9 | async-start | bytes 11489280 | tf_op jit(solution)/shard_map/all_gather | solution.py:121
  13.0 360.9 %all-gather.9.cloned.1.call-start = ((), (), s32[]{:S(2)}) async-start(), calls=%async_computation.4 | async-start | bytes 10340352 | tf_op jit(solution)/shard_map/all_gather | solution.py:121
  15.0 517.7 %reduce-scatter.13.cloned.1.call-start = ((), (), s32[]{:S(2)}) async-start(), calls=%async_computation.11 | async-start | bytes 10340352
  64.3 37.6 %copy-start.22 = (f32[128]{0:T(128)}, f32[128]{0:T(128)S(1)}, u32[]{:S(2)}) copy-start(f32[128]{0:T(128)S(1)} %broadcast_multiply_fusion.5) | copy-start | bytes 1540
  65.4 36.5 %copy-start.24 = (f32[128]{0:T(128)}, f32[128]{0:T(128)S(1)}, u32[]{:S(2)}) copy-start(f32[128]{0:T(128)S(1)} %add_rsqrt_fusion.1) | copy-start | bytes 1540
  66.1 35.8 %copy-start.6 = (bf16[128,1088]{0,1:T(8,128)(2,1)S(1)}, bf16[128,1088]{0,1:T(8,128)(2,1)}, u32[]{:S(2)}) copy-start(bf16[128,1088]{0,1:T(8,128)(2,1)} %param.8) | copy-start | bytes 835588
  108.4 4.2 copy-start.15
  108.8 169.7 %copy-start.11 = (bf16[128,1088]{0,1:T(8,128)(2,1)}, bf16[128,1088]{0,1:T(8,128)(2,1)S(1)}, u32[]{:S(2)}) copy-start(bf16[128,1088]{0,1:T(8,128)(2,1)S(1)} %get-tuple-element.50) | copy-start | bytes 835588
  109.7 58.6 %collective-permute-start = (bf16[2,128,1088]{1,2,0:T(8,128)(2,1)}, bf16[2,128,1088]{1,2,0:T(8,128)(2,1)}, u32[]{:S(2)}, u32[]{:S(2)}) collective-permute-start(bf16[2,128,1088]{1,2,0:T(8,128)(2,1)} %pad_maximum_fusion.1), channel_id=1, source_target_pairs={{0,1},{1,2},{2,3},{3,4},{4,5},{5,6},{6,7},{7,8},{8,9},{9,10},{10,1... | collective-permute-start | bytes 1671176 | tf_op jit(solution)/shard_map/ppermute | solution.py:22
  112.7 261.2 %copy-start.26 = (pred[128]{0:T(512)(128)(4,1)}, pred[128]{0:T(512)(128)(4,1)S(1)}, u32[]{:S(2)}) copy-start(pred[128]{0:T(512)(128)(4,1)S(1)} %iota_compare_fusion.1) | copy-start | bytes 388
  156.0 78.2 %collective-permute-start.5 = (bf16[2,128,1088]{1,2,0:T(8,128)(2,1)}, bf16[2,128,1088]{1,2,0:T(8,128)(2,1)S(1)}, u32[]{:S(2)}, u32[]{:S(2)}) collective-permute-start(bf16[2,128,1088]{1,2,0:T(8,128)(2,1)} %pad_maximum_fusion.1), channel_id=1, source_target_pairs={{0,6},{1,7},{2,8},{3,9},{4,10},{5,11},{6,12},{7,13},{8,14},{9,15},... | collective-permute-start | bytes 1671176 | tf_op jit(solution)/shard_map/ppermute | solution.py:22
  159.4 74.7 %collective-permute-start.4 = (bf16[2,128,1088]{1,2,0:T(8,128)(2,1)}, bf16[2,128,1088]{1,2,0:T(8,128)(2,1)S(1)}, u32[]{:S(2)}, u32[]{:S(2)}) collective-permute-start(bf16[2,128,1088]{1,2,0:T(8,128)(2,1)} %pad_maximum_fusion.1), channel_id=1, source_target_pairs={{0,5},{1,6},{2,7},{3,8},{4,9},{5,10},{6,11},{7,12},{8,13},{9,14},{... | collective-permute-start | bytes 1671176 | tf_op jit(solution)/shard_map/ppermute | solution.py:22
  162.1 71.9 %collective-permute-start.3 = (bf16[2,128,1088]{1,2,0:T(8,128)(2,1)}, bf16[2,128,1088]{1,2,0:T(8,128)(2,1)S(1)}, u32[]{:S(2)}, u32[]{:S(2)}) collective-permute-start(bf16[2,128,1088]{1,2,0:T(8,128)(2,1)} %pad_maximum_fusion.1), channel_id=1, source_target_pairs={{0,4},{1,5},{2,6},{3,7},{4,8},{5,9},{6,10},{7,11},{8,12},{9,13},{1... | collective-permute-start | bytes 1671176 | tf_op jit(solution)/shard_map/ppermute | solution.py:22
  164.6 22.5 %collective-permute-start.1 = (bf16[2,128,1088]{1,2,0:T(8,128)(2,1)}, bf16[2,128,1088]{1,2,0:T(8,128)(2,1)S(1)}, u32[]{:S(2)}, u32[]{:S(2)}) collective-permute-start(bf16[2,128,1088]{1,2,0:T(8,128)(2,1)} %pad_maximum_fusion.1), channel_id=1, source_target_pairs={{0,2},{1,3},{2,4},{3,5},{4,6},{5,7},{6,8},{7,9},{8,10},{9,11},{10,... | collective-permute-start | bytes 1671176 | tf_op jit(solution)/shard_map/ppermute | solution.py:22
  168.4 65.5 %collective-permute-start.2 = (bf16[2,128,1088]{1,2,0:T(8,128)(2,1)}, bf16[2,128,1088]{1,2,0:T(8,128)(2,1)S(1)}, u32[]{:S(2)}, u32[]{:S(2)}) collective-permute-start(bf16[2,128,1088]{1,2,0:T(8,128)(2,1)} %pad_maximum_fusion.1), channel_id=1, source_target_pairs={{0,3},{1,4},{2,5},{3,6},{4,7},{5,8},{6,9},{7,10},{8,11},{9,12},{10... | collective-permute-start | bytes 1671176 | tf_op jit(solution)/shard_map/ppermute | solution.py:22
  187.1 65.9 %collective-permute-start.6 = (bf16[2,128,1088]{1,2,0:T(8,128)(2,1)}, bf16[2,128,1088]{1,2,0:T(8,128)(2,1)S(1)}, u32[]{:S(2)}, u32[]{:S(2)}) collective-permute-start(bf16[2,128,1088]{1,2,0:T(8,128)(2,1)} %pad_maximum_fusion.1), channel_id=1, source_target_pairs={{0,7},{1,8},{2,9},{3,10},{4,11},{5,12},{6,13},{7,14},{8,15},{9,16}... | collective-permute-start | bytes 1671176 | tf_op jit(solution)/shard_map/ppermute | solution.py:22
  281.7 3.8 copy-start.1
  281.7 3.8 copy-start.7
  289.9 92.2 %copy-start.20 = (f32[128]{0:T(128)}, f32[128]{0:T(128)S(1)}, u32[]{:S(2)}) copy-start(f32[128]{0:T(128)S(1)} %add_rsqrt_fusion) | copy-start | bytes 1540
  373.9 8.1 copy-start
  382.1 2.8 copy-start.27
  384.9 2.8 copy-start.14
  386.1 3.8 copy-start.21
  390.0 5.5 copy-start.2
  400.9 247.4 %reduce-scatter.15.cloned.1.call-start = ((), (), s32[]{:S(2)}) async-start(), calls=%async_computation.12 | async-start | bytes 3041280
  405.3 400.3 %reduce-scatter.9.cloned.1.call-start = ((), (), s32[]{:S(2)}) async-start(), calls=%async_computation.5 | async-start | bytes 11489280 | tf_op jit(solution)/shard_map/reduce_scatter | solution.py:131
  416.6 513.6 %all-reduce.6.cloned.1.call-start = ((), (), s32[]{:S(2)}) async-start(), calls=%async_computation.10 | async-start | bytes 131072
  418.6 8.1 copy-start.4
  426.7 5.6 slice-start
  426.7 5.6 slice-start.1
  429.2 4.0 slice-start.2
  534.8 3.6 copy-start.5
  541.1 3.5 copy-start.3
  544.5 22.3 %copy-start.19 = (f32[4352]{0:T(1024)S(1)}, f32[4352]{0:T(1024)}, u32[]{:S(2)}) copy-start(f32[4352]{0:T(1024)} %get-tuple-element.71) | copy-start | bytes 52228
  546.1 6.5 collective-permute-start.7
  547.4 17.9 %collective-permute-start.13 = (bf16[2,128,1088]{1,2,0:T(8,128)(2,1)S(1)}, bf16[2,128,1088]{1,2,0:T(8,128)(2,1)}, u32[]{:S(2)}, u32[]{:S(2)}) collective-permute-start(bf16[2,128,1088]{1,2,0:T(8,128)(2,1)S(1)} %get-tuple-element.42), channel_id=1, source_target_pairs={{7,0},{8,1},{9,2},{10,3},{11,4},{12,5},{13,6},{14,7},{15,8},{16,9}... | collective-permute-start | bytes 1671176 | tf_op jit(solution)/shard_map/ppermute | solution.py:22
  548.7 102.6 %collective-permute-start.12 = (bf16[2,128,1088]{1,2,0:T(8,128)(2,1)}, bf16[2,128,1088]{1,2,0:T(8,128)(2,1)}, u32[]{:S(2)}, u32[]{:S(2)}) collective-permute-start(bf16[2,128,1088]{1,2,0:T(8,128)(2,1)} %get-tuple-element.43), channel_id=1, source_target_pairs={{6,0},{7,1},{8,2},{9,3},{10,4},{11,5},{12,6},{13,7},{14,8},{15,9},... | collective-permute-start | bytes 1671176 | tf_op jit(solution)/shard_map/ppermute | solution.py:22
  550.0 101.3 %collective-permute-start.11 = (bf16[2,128,1088]{1,2,0:T(8,128)(2,1)}, bf16[2,128,1088]{1,2,0:T(8,128)(2,1)}, u32[]{:S(2)}, u32[]{:S(2)}) collective-permute-start(bf16[2,128,1088]{1,2,0:T(8,128)(2,1)} %get-tuple-element.44), channel_id=1, source_target_pairs={{5,0},{6,1},{7,2},{8,3},{9,4},{10,5},{11,6},{12,7},{13,8},{14,9},{... | collective-permute-start | bytes 1671176 | tf_op jit(solution)/shard_map/ppermute | solution.py:22
  551.3 100.0 %collective-permute-start.10 = (bf16[2,128,1088]{1,2,0:T(8,128)(2,1)}, bf16[2,128,1088]{1,2,0:T(8,128)(2,1)}, u32[]{:S(2)}, u32[]{:S(2)}) collective-permute-start(bf16[2,128,1088]{1,2,0:T(8,128)(2,1)} %get-tuple-element.45), channel_id=1, source_target_pairs={{4,0},{5,1},{6,2},{7,3},{8,4},{9,5},{10,6},{11,7},{12,8},{13,9},{1... | collective-permute-start | bytes 1671176 | tf_op jit(solution)/shard_map/ppermute | solution.py:22
  552.6 98.7 %collective-permute-start.9 = (bf16[2,128,1088]{1,2,0:T(8,128)(2,1)}, bf16[2,128,1088]{1,2,0:T(8,128)(2,1)}, u32[]{:S(2)}, u32[]{:S(2)}) collective-permute-start(bf16[2,128,1088]{1,2,0:T(8,128)(2,1)} %get-tuple-element.46), channel_id=1, source_target_pairs={{3,0},{4,1},{5,2},{6,3},{7,4},{8,5},{9,6},{10,7},{11,8},{12,9},{13... | collective-permute-start | bytes 1671176 | tf_op jit(solution)/shard_map/ppermute | solution.py:22
  565.3 86.0 %collective-permute-start.8 = (bf16[2,128,1088]{1,2,0:T(8,128)(2,1)}, bf16[2,128,1088]{1,2,0:T(8,128)(2,1)}, u32[]{:S(2)}, u32[]{:S(2)}) collective-permute-start(bf16[2,128,1088]{1,2,0:T(8,128)(2,1)} %get-tuple-element.47), channel_id=1, source_target_pairs={{2,0},{3,1},{4,2},{5,3},{6,4},{7,5},{8,6},{9,7},{10,8},{11,9},{12,... | collective-permute-start | bytes 1671176 | tf_op jit(solution)/shard_map/ppermute | solution.py:22
  651.3 156.5 %copy-start.23 = (f32[128]{0:T(128)S(1)}, f32[128]{0:T(128)}, u32[]{:S(2)}) copy-start(f32[128]{0:T(128)} %copy-done.22) | copy-start | bytes 1540
  651.3 156.5 %copy-start.25 = (f32[128]{0:T(128)S(1)}, f32[128]{0:T(128)}, u32[]{:S(2)}) copy-start(f32[128]{0:T(128)} %copy-done.24) | copy-start | bytes 1540
  814.7 269.4 %reduce-scatter.11.cloned.1.call-start = ((), (), s32[]{:S(2)}) async-start(), calls=%async_computation.6 | async-start | bytes 8785920 | tf_op jit(solution)/shard_map/reduce_scatter | solution.py:131
  831.3 8.0 copy-start.9
  831.3 8.0 copy-start.17
  (7 other events, 10.0 us)
Sparse Core Ops, SparseCore 0:
  11.4 80.5 all-gather.10
  95.5 57.2 all-gather.12
  156.2 117.6 all-gather.14
  277.3 96.6 all-gather.8
  401.0 131.6 reduce-scatter.12
  538.0 110.2 reduce-scatter.14
  650.6 154.9 reduce-scatter.8
  814.9 115.2 all-reduce.5
  932.4 151.6 reduce-scatter.10
